TPU v7x, 32 devices: a whole 2x2x4 slice. The times are simulated.
32 devices in a mesh: req: 8 (over z, x), mp: 4 (over y, core).
Axes of the slice: x: 2, y: 2, z: 4, core: 2. Of those that a mesh axis runs over, the one named last changes fastest.
Arguments:
- hidden: bfloat16 [2048, 4096], P(('req', 'mp')), may hold values from -4 to 4
- queries: bfloat16 [2048, 2048], P('req', 'mp'), may hold values from -130 to 130
- rotated_rollout_keys: bfloat16 [2048, 2, 128], P('req'), may hold values from -4 to 4
- rollout_value_matrix: bfloat16 [2048, 2, 128], P('req'), may hold values from -4 to 4
- cached_key_slabs: bfloat16 [16384, 2, 128], P('req'), may hold values from -4 to 4
- cached_value_slabs: bfloat16 [16384, 2, 128], P('req'), may hold values from -4 to 4
- out_weight: bfloat16 [2048, 4096], P('mp'), may hold values from -0.5 to 0.5
- final_gain: float32 [4096], replicated, may hold values from 0.1 to 1.9
- head_weight: bfloat16 [4096, 32000], P(None, 'req'), may hold values from -1 to 1
- token_ids: int32 [2048], P(('req', 'mp')), may hold values from 0 to 31999
- rollout_len: int32 [8], P('req'), may hold values from 64 to 256
- piece_offset: int32 [8], P('req'), may hold values from 0 to 3
- piece_len: int32 [8], P('req'), may hold values from 256 to 2048
Outputs:
- logprob: float32 [2048], P(('req', 'mp'))
- entropy: float32 [2048], P(('req', 'mp'))
All inputs are finite; a program needn't handle non-finite values.
Results may differ from a plain program's by a relative error of at most 0.0045.
Values may be sent and summed in bfloat16 or wider, within the bound.
No kernel may reach another device: no remote copies, remote signals or barrier semaphores. Data moves between devices by JAX's collectives and lax.ppermute only.
A program may use at most 128 MiB of HBM per device.

v0:
```python
import math
import jax
import jax.numpy as jnp
from jax import lax
from jax.sharding import PartitionSpec as P

REACH = 4
NEGATIVE = -1e30


def shifted(block, axis, distance):
    devices = range(lax.axis_size(axis))
    route = [((i - distance) % len(devices), i) for i in devices]
    return lax.ppermute(block, axis, route)


def combined_all(shard, axis, combine):
    everything = jax.tree.map(lambda part: lax.all_gather(part, axis), shard)
    leading = jax.tree.map(lambda part: part[0], everything)

    def hop(k, so_far):
        return combine(so_far, jax.tree.map(lambda part: part[k], everything))

    return lax.fori_loop(1, lax.axis_size(axis), hop, leading)


def partial_softmax(query, keys, values, mask, factor):
    scores = jnp.einsum("thd,cd->thc", query, keys, preferred_element_type=jnp.float32) * factor
    scores = jnp.where(mask[:, None, :], scores, NEGATIVE)
    top = jnp.max(scores, axis=-1)
    weights = jnp.exp(scores - top[..., None])
    total = jnp.sum(weights, axis=-1)
    summed = jnp.einsum(
        "thc,cd->thd", weights.astype(jnp.bfloat16), values, preferred_element_type=jnp.float32
    )
    return (top, total, summed)


def join_parts(parts):
    tops = jnp.concatenate([item[0] for item in parts], axis=0)
    totals = jnp.concatenate([item[1] for item in parts], axis=0)
    sums = jnp.concatenate([item[2] for item in parts], axis=0)
    highest = jnp.max(tops, axis=0)
    scales = jnp.exp(tops - highest[None])
    total = jnp.sum(totals * scales, axis=0)
    summed = jnp.einsum("nth,nthd->thd", scales, sums)
    return summed / total[..., None]


def merge_summary(leading_slab, second):
    highest = jnp.maximum(leading_slab[0], second[0])
    left = jnp.exp(leading_slab[0] - highest)
    right = jnp.exp(second[0] - highest)
    return (
        highest,
        leading_slab[1] * left + second[1] * right,
        leading_slab[2] * left + second[2] * right,
        leading_slab[3] + second[3],
    )


def body(
    hidden,
    queries,
    rotated_rollout_keys,
    rollout_value_matrix,
    cached_key_slabs,
    cached_value_slabs,
    out_weight,
    final_gain,
    head_weight,
    token_ids,
    rollout_len,
    piece_offset,
    piece_len,
):
    groups = lax.axis_size("req")
    request = lax.axis_index("req")
    shard = lax.axis_index("mp")
    rollout = queries.shape[0]
    head_size = rotated_rollout_keys.shape[2]
    heads_here = queries.shape[1] // head_size
    group_size = heads_here * lax.axis_size("mp") // rotated_rollout_keys.shape[1]
    value_head = shard * heads_here // group_size
    factor = 1.0 / math.sqrt(head_size)
    offset = piece_offset[0]
    current_slab_keys = lax.dynamic_index_in_dim(cached_key_slabs, value_head, 1, keepdims=False)
    current_slab_values = lax.dynamic_index_in_dim(
        cached_value_slabs, value_head, 1, keepdims=False
    )
    slab_valid = jnp.arange(cached_key_slabs.shape[0]) < piece_len[0]
    rollout_key_rows = lax.dynamic_index_in_dim(rotated_rollout_keys, value_head, 1, keepdims=False)
    rollout_value_rows = lax.dynamic_index_in_dim(
        rollout_value_matrix, value_head, 1, keepdims=False
    )
    rows = jnp.arange(rollout)
    causal = rows[None, :] <= rows[:, None]
    own_query = queries.reshape(rollout, heads_here, head_size)
    local = partial_softmax(own_query, rollout_key_rows, rollout_value_rows, causal, factor)
    parts = [tuple((item[None] for item in local))]
    slab_mask = jnp.broadcast_to(slab_valid, (rollout, cached_key_slabs.shape[0]))
    visitor = queries
    for step in range(1, REACH):
        moved = shifted(queries, "req", step)
        visitor = jnp.where(offset == step, moved, visitor)
    top, total, summed = partial_softmax(
        visitor.reshape(rollout, heads_here, head_size),
        current_slab_keys,
        current_slab_values,
        slab_mask,
        factor,
    )
    keep = offset == 0
    parts.append(
        (
            jnp.where(keep, top, NEGATIVE)[None],
            jnp.where(keep, total, 0.0)[None],
            jnp.where(keep, summed, 0.0)[None],
        )
    )
    for step in range(1, REACH):
        mine = offset == step
        back_sum, back_top, back_total = shifted(
            (
                jnp.where(mine, summed, 0.0),
                jnp.where(mine, top, NEGATIVE),
                jnp.where(mine, total, 0.0),
            ),
            "req",
            -step,
        )
        parts.append((back_top[None], back_total[None], back_sum[None]))
    mixed = join_parts(parts).astype(jnp.bfloat16).reshape(rollout, heads_here * head_size)
    rows_here = hidden.shape[0]
    block = mixed
    added = lax.psum_scatter(
        jnp.dot(block, out_weight, preferred_element_type=jnp.float32),
        "mp",
        scatter_dimension=0,
        tiled=True,
    )
    stream = hidden.astype(jnp.float32) + added
    normed = (
        stream * lax.rsqrt(jnp.mean(stream * stream, axis=-1, keepdims=True) + 1e-06) * final_gain
    ).astype(jnp.bfloat16)
    vocabulary_here = head_weight.shape[1]
    first_word = request * vocabulary_here
    columns = jnp.arange(vocabulary_here)
    block = lax.all_gather(normed, "req", axis=0, tiled=True)
    words = lax.all_gather(token_ids, "req", axis=0, tiled=True)
    logits = jnp.dot(block, head_weight, preferred_element_type=jnp.float32)
    highest = jnp.max(logits, axis=-1)
    spread = jnp.exp(logits - highest[:, None])
    total = jnp.sum(spread, axis=-1)
    weighted = jnp.sum(spread * logits, axis=-1)
    picked = jnp.sum(
        jnp.where(columns[None, :] == (words - first_word)[:, None], logits, 0.0), axis=-1
    )
    fresh = (highest, total, weighted, picked)
    summary = tuple((fresh[index] for index in range(4)))
    table = tuple((item.reshape(groups, rows_here) for item in summary))
    pooled = combined_all(table, "req", merge_summary)
    highest, total, weighted, picked = (
        lax.dynamic_index_in_dim(item, request, 0, keepdims=False) for item in pooled
    )
    log_total = highest + jnp.log(total)
    positions = shard * rows_here + jnp.arange(rows_here)
    valid = positions < rollout_len[0]
    logprob = jnp.where(valid, picked - log_total, 0.0)
    entropy = jnp.where(valid, log_total - weighted / total, 0.0)
    return (logprob, entropy)


def solution(mesh):
    placed = (
        P(("req", "mp"), None),
        P("req", "mp"),
        P("req", None, None),
        P("req", None, None),
        P("req", None, None),
        P("req", None, None),
        P("mp", None),
        P(),
        P(None, "req"),
        P(("req", "mp")),
        P("req"),
        P("req"),
        P("req"),
    )
    return jax.shard_map(
        body,
        mesh=mesh,
        in_specs=placed,
        out_specs=(P(("req", "mp")), P(("req", "mp"))),
        check_vma=False,
    )
```

profile of v0, /device:TPU:0, one launch (start us, length us, event | category | flops | bytes accessed | tf_op | source)
XLA Modules:
  0.0 363.0 jit_solution(10148285551743144967)
XLA Ops:
  7.2 4.0 %collective-permute-start = (bf16[256,512]{1,0:T(8,128)(2,1)}, bf16[256,512]{1,0:T(8,128)(2,1)S(1)}, u32[]{:S(2)}, u32[]{:S(2)}) collective-permute-start(bf16[256,512]{1,0:T(8,128)(2,1)} %param.16), channel_id=1, source_target_pairs={{20,0},{24,4},{28,8},{0,12},{4,16},{8,20},{12,24},{16,28},{21,1},{... | collective-permute-start | bytes 786440 | tf_op jit(solution)/shard_map/ppermute | solution.py:14
  11.2 1.6 collective-permute-start.1
  12.8 1.5 collective-permute-start.2
  15.7 1.1 constant_dynamic-slice_fusion.6
  17.9 1.3 fusion.34
  20.5 2.2 constant_dynamic-slice_fusion.4
  23.0 12.6 %collective-permute-done = bf16[256,512]{1,0:T(8,128)(2,1)S(1)} collective-permute-done((bf16[256,512]{1,0:T(8,128)(2,1)}, bf16[256,512]{1,0:T(8,128)(2,1)S(1)}, u32[]{:S(2)}, u32[]{:S(2)}) %collective-permute-start) | collective-permute-done | bytes 262176 | tf_op jit(solution)/shard_map/ppermute | solution.py:14
  35.6 1.6 fusion.4
  37.2 1.9 fusion.5
  39.2 1.1 collective-permute-start.10
  40.3 3.0 collective-permute-start.11
  43.3 1.5 collective-permute-start.3
  45.1 2.0 bitcast_dynamic-update-slice_fusion.3
  47.3 3.2 collective-permute-start.5
  50.5 1.9 collective-permute-start.6
  52.4 2.7 collective-permute-start.7
  56.7 2.4 collective-permute-done.6
  59.2 5.6 %collective-permute-done.7 = bf16[256,4,128]{2,0,1:T(8,128)(2,1)S(1)} collective-permute-done((bf16[256,4,128]{2,0,1:T(8,128)(2,1)S(1)}, bf16[256,4,128]{2,0,1:T(8,128)(2,1)S(1)}, u32[]{:S(2)}, u32[]{:S(2)}) %collective-permute-start.7) | collective-permute-done | bytes 262176 | tf_op jit(solution)/shard_map/ppermute | solution.py:14
  64.8 3.2 collective-permute-done.8
  68.1 1.3 fusion.7
  69.8 5.4 %fusion.20 = f32[256,4096]{1,0:T(8,128)} fusion(bf16[512,4096]{1,0:T(8,128)(2,1)} %param.21, bf16[32,8,4,128]{3,2,1,0:T(4,128)(2,1)S(1)} %bitcast.137), kind=kOutput, calls=%fused_computation.43 | convolution fusion | flops 1073741824 | bytes 8650752 | tf_op jit(solution)/shard_map/dot_general | solution.py:137
  75.5 51.9 %reduce-scatter.2.cloned.1.call-done = f32[64,4096]{1,0:T(8,128)} async-done(((f32[256,4096]{1,0:T(8,128)}), f32[64,4096]{1,0:T(8,128)}) %reduce-scatter.2.cloned.1.call-update) | async-done | bytes 1048592 | tf_op jit(solution)/shard_map/reduce_scatter | solution.py:136
  127.4 1.5 multiply_reduce_fusion.1
  128.9 2.2 multiply_convert_fusion
  133.3 11.8 %all-reduce = s32[512]{0:T(512)S(1)} all-reduce(s32[512]{0:T(512)S(1)} %dynamic-update-slice), channel_id=1, replica_groups=mesh['req'=8,'mp'=4] {'req'}, use_global_device_ids=true, to_apply=%add | all-reduce | flops 512 | bytes 4096
  145.1 59.6 %all-gather.2.cloned.1.call-done = bf16[512,4096]{1,0:T(8,128)(2,1)} async-done(((bf16[64,4096]{1,0:T(8,128)(2,1)}), bf16[512,4096]{1,0:T(8,128)(2,1)}) %all-gather.2.cloned.1.call-update) | async-done | bytes 4194320 | tf_op jit(solution)/shard_map/all_gather | solution.py:149
  204.7 23.6 %fusion.35 = (f32[512]{0:T(512)S(1)}, f32[512,4000]{0,1:T(8,128)}) fusion(bf16[512,4096]{1,0:T(8,128)(2,1)} %all-gather.2.cloned.1.call-done, bf16[4096,4000]{0,1:T(8,128)(2,1)} %param.23), kind=kOutput, calls=%fused_computation.102 | convolution fusion | flops 16779264000 | bytes 45156352 | tf_op jit(solution)/shard_map/dot_general | solution.py:151
  228.4 4.8 %multiply_reduce_fusion = (f32[512]{0:T(512)S(1)}, f32[512]{0:T(512)S(1)}, f32[512]{0:T(512)S(1)}) fusion(f32[512,4000]{0,1:T(8,128)} %get-tuple-element.271, f32[512]{0:T(512)S(1)} %get-tuple-element.270, s32[512]{0:T(512)S(1)} %broadcast_subtract_fusion), kind=kLoop, calls=%fused_computation.13 | loop fusion | flops 14334464 | bytes 8202240 | tf_op jit(solution)/shard_map/reduce_sum | solution.py:155
  233.3 30.4 %all_gather.23 = f32[8,8,64]{2,1,0:T(8,128)S(1)} all-gather(f32[1,8,64]{2,1,0:T(8,128)S(1)} %all_gather_reshape.15), channel_id=1, replica_groups=mesh['req'=8,'mp'=4] {'req'}, dimensions={0}, use_global_device_ids=true | all-gather | bytes 18432 | tf_op jit(solution)/shard_map/all_gather | solution.py:18
  263.8 30.4 %all_gather.21 = f32[8,8,64]{2,1,0:T(8,128)S(1)} all-gather(f32[1,8,64]{2,1,0:T(8,128)S(1)} %all_gather_reshape.14), channel_id=1, replica_groups=mesh['req'=8,'mp'=4] {'req'}, dimensions={0}, use_global_device_ids=true | all-gather | bytes 18432 | tf_op jit(solution)/shard_map/all_gather | solution.py:18
  294.3 30.4 %all_gather.20 = f32[8,8,64]{2,1,0:T(8,128)S(1)} all-gather(f32[1,8,64]{2,1,0:T(8,128)S(1)} %all_gather_reshape.13), channel_id=1, replica_groups=mesh['req'=8,'mp'=4] {'req'}, dimensions={0}, use_global_device_ids=true | all-gather | bytes 18432 | tf_op jit(solution)/shard_map/all_gather | solution.py:18
  324.7 30.4 %all_gather.19 = f32[8,8,64]{2,1,0:T(8,128)S(1)} all-gather(f32[1,8,64]{2,1,0:T(8,128)S(1)} %all_gather_reshape.12), channel_id=1, replica_groups=mesh['req'=8,'mp'=4] {'req'}, dimensions={0}, use_global_device_ids=true | all-gather | bytes 18432 | tf_op jit(solution)/shard_map/all_gather | solution.py:18
  (93 shorter events, 8.2 us)
Async XLA Ops:
  7.2 8.6 %copy-start = (bf16[2048,2,128]{2,1,0:T(2,128)(2,1)S(1)}, bf16[2048,2,128]{2,1,0:T(2,128)(2,1)}, u32[]{:S(2)}) copy-start(bf16[2048,2,128]{2,1,0:T(2,128)(2,1)} %param.19) | copy-start | bytes 3145732
  7.2 28.5 %copy-start.3 = (bf16[256,512]{1,0:T(8,128)(2,1)S(1)}, bf16[256,512]{1,0:T(8,128)(2,1)}, u32[]{:S(2)}) copy-start(bf16[256,512]{1,0:T(8,128)(2,1)} %param.16) | copy-start | bytes 786436
  7.2 120.2 %reduce-scatter.2.cloned.1.call-start = ((), (), s32[]{:S(2)}) async-start(), calls=%async_computation.1 | async-start | bytes 5242880 | tf_op jit(solution)/shard_map/reduce_scatter | solution.py:136
  7.2 28.4 %collective-permute-start = (bf16[256,512]{1,0:T(8,128)(2,1)}, bf16[256,512]{1,0:T(8,128)(2,1)S(1)}, u32[]{:S(2)}, u32[]{:S(2)}) collective-permute-start(bf16[256,512]{1,0:T(8,128)(2,1)} %param.16), channel_id=1, source_target_pairs={{20,0},{24,4},{28,8},{0,12},{4,16},{8,20},{12,24},{16,28},{21,1},{... | collective-permute-start | bytes 786440 | tf_op jit(solution)/shard_map/ppermute | solution.py:14
  11.2 24.4 %collective-permute-start.1 = (bf16[256,512]{1,0:T(8,128)(2,1)}, bf16[256,512]{1,0:T(8,128)(2,1)S(1)}, u32[]{:S(2)}, u32[]{:S(2)}) collective-permute-start(bf16[256,512]{1,0:T(8,128)(2,1)} %param.16), channel_id=1, source_target_pairs={{24,0},{28,4},{0,8},{4,12},{8,16},{12,20},{16,24},{20,28},{25,1},{... | collective-permute-start | bytes 786440 | tf_op jit(solution)/shard_map/ppermute | solution.py:14
  12.8 22.8 %collective-permute-start.2 = (bf16[256,512]{1,0:T(8,128)(2,1)}, bf16[256,512]{1,0:T(8,128)(2,1)S(1)}, u32[]{:S(2)}, u32[]{:S(2)}) collective-permute-start(bf16[256,512]{1,0:T(8,128)(2,1)} %param.16), channel_id=1, source_target_pairs={{28,0},{0,4},{4,8},{8,12},{12,16},{16,20},{20,24},{24,28},{29,1},{... | collective-permute-start | bytes 786440 | tf_op jit(solution)/shard_map/ppermute | solution.py:14
  39.1 16.0 %collective-permute-start.9 = (f32[256,4]{0,1:T(4,128)S(1)}, f32[256,4]{0,1:T(4,128)S(1)}, u32[]{:S(2)}, u32[]{:S(2)}) collective-permute-start(f32[256,4]{0,1:T(4,128)S(1)} %get-tuple-element.260), channel_id=1, source_target_pairs={{4,0},{8,4},{12,8},{16,12},{20,16},{24,20},{28,24},{0,28},{5,1},{9... | collective-permute-start | bytes 12296 | tf_op jit(solution)/shard_map/ppermute | solution.py:14
  39.2 16.9 %collective-permute-start.10 = (f32[256,4]{0,1:T(4,128)S(1)}, f32[256,4]{0,1:T(4,128)S(1)}, u32[]{:S(2)}, u32[]{:S(2)}) collective-permute-start(f32[256,4]{0,1:T(4,128)S(1)} %get-tuple-element.259), channel_id=1, source_target_pairs={{8,0},{12,4},{16,8},{20,12},{24,16},{28,20},{0,24},{4,28},{9,1},{1... | collective-permute-start | bytes 12296 | tf_op jit(solution)/shard_map/ppermute | solution.py:14
  40.3 15.8 %collective-permute-start.11 = (f32[256,4]{0,1:T(4,128)S(1)}, f32[256,4]{0,1:T(4,128)S(1)}, u32[]{:S(2)}, u32[]{:S(2)}) collective-permute-start(f32[256,4]{0,1:T(4,128)S(1)} %get-tuple-element.258), channel_id=1, source_target_pairs={{12,0},{16,4},{20,8},{24,12},{28,16},{0,20},{4,24},{8,28},{13,1},{... | collective-permute-start | bytes 12296 | tf_op jit(solution)/shard_map/ppermute | solution.py:14
  43.3 4.0 %collective-permute-start.3 = (f32[256,4]{0,1:T(4,128)S(1)}, f32[256,4]{0,1:T(4,128)S(1)}, u32[]{:S(2)}, u32[]{:S(2)}) collective-permute-start(f32[256,4]{0,1:T(4,128)S(1)} %get-tuple-element.263), channel_id=1, source_target_pairs={{4,0},{8,4},{12,8},{16,12},{20,16},{24,20},{28,24},{0,28},{5,1},{9... | collective-permute-start | bytes 12296 | tf_op jit(solution)/shard_map/ppermute | solution.py:14
  44.8 5.7 %collective-permute-start.4 = (f32[256,4]{0,1:T(4,128)S(1)}, f32[256,4]{0,1:T(4,128)S(1)}, u32[]{:S(2)}, u32[]{:S(2)}) collective-permute-start(f32[256,4]{0,1:T(4,128)S(1)} %get-tuple-element.262), channel_id=1, source_target_pairs={{8,0},{12,4},{16,8},{20,12},{24,16},{28,20},{0,24},{4,28},{9,1},{1... | collective-permute-start | bytes 12296 | tf_op jit(solution)/shard_map/ppermute | solution.py:14
  47.3 5.1 %collective-permute-start.5 = (f32[256,4]{0,1:T(4,128)S(1)}, f32[256,4]{0,1:T(4,128)S(1)}, u32[]{:S(2)}, u32[]{:S(2)}) collective-permute-start(f32[256,4]{0,1:T(4,128)S(1)} %get-tuple-element.261), channel_id=1, source_target_pairs={{12,0},{16,4},{20,8},{24,12},{28,16},{0,20},{4,24},{8,28},{13,1},{... | collective-permute-start | bytes 12296 | tf_op jit(solution)/shard_map/ppermute | solution.py:14
  50.5 8.7 %collective-permute-start.6 = (bf16[256,4,128]{2,0,1:T(8,128)(2,1)S(1)}, bf16[256,4,128]{2,0,1:T(8,128)(2,1)S(1)}, u32[]{:S(2)}, u32[]{:S(2)}) collective-permute-start(bf16[256,4,128]{2,0,1:T(8,128)(2,1)S(1)} %get-tuple-element.255), channel_id=1, source_target_pairs={{4,0},{8,4},{12,8},{16,12},{20,16},{24,20},{28,24},{0,28},{5,1},{9... | collective-permute-start | bytes 786440 | tf_op jit(solution)/shard_map/ppermute | solution.py:14
  52.4 12.4 %collective-permute-start.7 = (bf16[256,4,128]{2,0,1:T(8,128)(2,1)S(1)}, bf16[256,4,128]{2,0,1:T(8,128)(2,1)S(1)}, u32[]{:S(2)}, u32[]{:S(2)}) collective-permute-start(bf16[256,4,128]{2,0,1:T(8,128)(2,1)S(1)} %get-tuple-element.254), channel_id=1, source_target_pairs={{8,0},{12,4},{16,8},{20,12},{24,16},{28,20},{0,24},{4,28},{9,1},{1... | collective-permute-start | bytes 786440 | tf_op jit(solution)/shard_map/ppermute | solution.py:14
  55.1 12.9 %collective-permute-start.8 = (bf16[256,4,128]{2,0,1:T(8,128)(2,1)S(1)}, bf16[256,4,128]{2,0,1:T(8,128)(2,1)S(1)}, u32[]{:S(2)}, u32[]{:S(2)}) collective-permute-start(bf16[256,4,128]{2,0,1:T(8,128)(2,1)S(1)} %get-tuple-element.253), channel_id=1, source_target_pairs={{12,0},{16,4},{20,8},{24,12},{28,16},{0,20},{4,24},{8,28},{13,1},{... | collective-permute-start | bytes 786440 | tf_op jit(solution)/shard_map/ppermute | solution.py:14
  69.4 58.0 %copy-start.2 = (bf16[64,4096]{1,0:T(8,128)(2,1)S(1)}, bf16[64,4096]{1,0:T(8,128)(2,1)}, u32[]{:S(2)}) copy-start(bf16[64,4096]{1,0:T(8,128)(2,1)} %param.15) | copy-start | bytes 1572868
  69.8 59.1 %copy-start.4 = (f32[4096]{0:T(1024)S(1)}, f32[4096]{0:T(1024)}, u32[]{:S(2)}) copy-start(f32[4096]{0:T(1024)} %param.22) | copy-start | bytes 49156
  69.8 62.0 %copy-start.6 = (u32[32]{0:T(128)S(1)}, u32[32]{0:T(128)}, u32[]{:S(2)}) copy-start(u32[32]{0:T(128)} %constant.121) | copy-start | bytes 388
  69.8 63.2 %copy-start.5 = (s32[64]{0:T(128)S(1)}, s32[64]{0:T(128)}, u32[]{:S(2)}) copy-start(s32[64]{0:T(128)} %param.24) | copy-start | bytes 772
  75.2 129.4 %all-gather.2.cloned.1.call-start = ((), (), s32[]{:S(2)}) async-start(), calls=%async_computation.2 | async-start | bytes 4718592 | tf_op jit(solution)/shard_map/all_gather | solution.py:149
  204.7 151.5 %copy-start.1 = (bf16[2048,2,128]{2,1,0:T(2,128)(2,1)S(1)}, bf16[2048,2,128]{2,1,0:T(2,128)(2,1)}, u32[]{:S(2)}) copy-start(bf16[2048,2,128]{2,1,0:T(2,128)(2,1)} %param.19) | copy-start | bytes 3145732
Sparse Core Ops, SparseCore 0:
  75.4 51.9 reduce-scatter.1
  131.2 73.3 all-gather.1
where the time goes:
time: 363 us
  waiting for transfers between devices  135 us (37%)
  blocking collectives  133 us (37%)
  matrix products  35.6 us (10%)
  starting transfers between devices  22.1 us (6%)
  between operations  17 us (5%)
  other arithmetic  12 us (3%)
  local copies, waits for them, and re-layouts  7.34 us (2%)
    all_gather x4, blocking collectives, combined_all(): everything = jax.tree.map(lambda part: lax.all_gather(part, axis), shard)  122 us
    all_gather x1, waiting for transfers between devices, body(): block = lax.all_gather(normed, 'req', axis=0, tiled=True)  59.6 us
    reduce_scatter x1, waiting for transfers between devices, body(): lax.psum_scatter(jnp.dot(block, out_weight, preferred_element_type=jnp.fl...  51.9 us
    ppermute x12, waiting for transfers between devices, shifted(): return lax.ppermute(block, axis, route)  23.8 us
    dot_general x1, matrix products, body(): logits = jnp.dot(block, head_weight, preferred_element_type=jnp.float32)  23.6 us
    ppermute x12, starting transfers between devices, shifted(): return lax.ppermute(block, axis, route)  21.8 us
    unnamed x1, blocking collectives  11.8 us
  transfers between devices with their start and end apart: 14, of which 6 were waited for; matrix products, arithmetic and copies ran while one was open for 3% of the time, Pallas kernels for 0%

commit v1 on v0

--- a/solution.py
+++ b/solution.py
@@ -146,7 +146,16 @@
     vocabulary_here = head_weight.shape[1]
     first_word = request * vocabulary_here
     columns = jnp.arange(vocabulary_here)
-    block = lax.all_gather(normed, "req", axis=0, tiled=True)
+    n_peers_all = lax.axis_size("req")
+    so_far_all = [(nth, (nth + 1) % n_peers_all) for nth in range(n_peers_all)]
+    block_next, y_new = ([normed], [normed])
+    rack = [(nth, (nth - 1) % n_peers_all) for nth in range(n_peers_all)]
+    for _ in range(n_peers_all // 2):
+        block_next.append(lax.ppermute(block_next[-1], "req", so_far_all))
+    for _ in range((n_peers_all - 1) // 2):
+        y_new.append(lax.ppermute(y_new[-1], "req", rack))
+    all_rows = jnp.concatenate([*block_next[::-1], *y_new[1:]], axis=0)
+    block = jnp.roll(all_rows, (lax.axis_index("req") - n_peers_all // 2) * normed.shape[0], axis=0)
     words = lax.all_gather(token_ids, "req", axis=0, tiled=True)
     logits = jnp.dot(block, head_weight, preferred_element_type=jnp.float32)
     highest = jnp.max(logits, axis=-1)

time: 363 us -> 386 us (1.063)
  starting transfers between devices: 22.1 us -> 46.2 us
  waiting for transfers between devices: 135 us -> 127 us
  blocking collectives: 133 us -> 138 us
    all_gather x1 -> x0, waiting for transfers between devices: 59.6 us -> none  [body(): block = lax.all_gather(normed, 'req', axis=0, tiled=True)]
    ppermute x0 -> x7, waiting for transfers between devices: none -> 50.7 us  [the longest x4 40.6 us: body(): block_next.append(lax.ppermute(block_next[-1], 'req', so_far_all))]
    ppermute x0 -> x7, starting transfers between devices: none -> 24.3 us  [the longest x3 17.7 us: body(): y_new.append(lax.ppermute(y_new[-1], 'req', rack))]
    unnamed x1, blocking collectives: 11.8 us -> 16.6 us
  transfers between devices with their start and end apart: 14 -> 20, of which waited for: 6 -> 9; matrix products, arithmetic and copies ran while one was open for 3% -> 3% of each run, Pallas kernels for 0% -> 0%
where the time goes in v1:
time: 386 us; the launch traced here: 385 us
  blocking collectives  138 us (36%)
  waiting for transfers between devices  127 us (33%)
  starting transfers between devices  46.2 us (12%)
  matrix products  35.6 us (9%)
  between operations  17.1 us (4%)
  other arithmetic  11.2 us (3%)
  local copies, waits for them, and re-layouts  10 us (3%)
    all_gather x4, blocking collectives, combined_all(): everything = jax.tree.map(lambda part: lax.all_gather(part, axis), shard)  122 us
    reduce_scatter x1, waiting for transfers between devices, body(): lax.psum_scatter(jnp.dot(block, out_weight, preferred_element_type=jnp.fl...  52.2 us
    ppermute x4, waiting for transfers between devices, body(): block_next.append(lax.ppermute(block_next[-1], 'req', so_far_all))  40.6 us
    ppermute x12, waiting for transfers between devices, shifted(): return lax.ppermute(block, axis, route)  23.8 us
    dot_general x1, matrix products, body(): logits = jnp.dot(block, head_weight, preferred_element_type=jnp.float32)  23.7 us
    ppermute x12, starting transfers between devices, shifted(): return lax.ppermute(block, axis, route)  21.8 us
    ppermute x3, starting transfers between devices, body(): y_new.append(lax.ppermute(y_new[-1], 'req', rack))  17.7 us
    unnamed x1, blocking collectives  16.6 us
  transfers between devices with their start and end apart: 20, of which 9 were waited for; matrix products, arithmetic and copies ran while one was open for 3% of the time, Pallas kernels for 0%

profile of v1, /device:TPU:0, one launch (start us, length us, event | category | flops | bytes accessed | tf_op | source)
XLA Modules:
  0.0 385.4 jit_solution(8319802722004875400)
XLA Ops:
  7.2 4.0 %collective-permute-start = (bf16[256,512]{1,0:T(8,128)(2,1)}, bf16[256,512]{1,0:T(8,128)(2,1)S(1)}, u32[]{:S(2)}, u32[]{:S(2)}) collective-permute-start(bf16[256,512]{1,0:T(8,128)(2,1)} %param.16), channel_id=1, source_target_pairs={{20,0},{24,4},{28,8},{0,12},{4,16},{8,20},{12,24},{16,28},{21,1},{... | collective-permute-start | bytes 786440 | tf_op jit(solution)/shard_map/ppermute | solution.py:14
  11.2 1.6 collective-permute-start.1
  20.5 2.2 constant_dynamic-slice_fusion.4
  23.0 12.6 %collective-permute-done = bf16[256,512]{1,0:T(8,128)(2,1)S(1)} collective-permute-done((bf16[256,512]{1,0:T(8,128)(2,1)}, bf16[256,512]{1,0:T(8,128)(2,1)S(1)}, u32[]{:S(2)}, u32[]{:S(2)}) %collective-permute-start) | collective-permute-done | bytes 262176 | tf_op jit(solution)/shard_map/ppermute | solution.py:14
  35.6 1.6 fusion.4
  37.2 1.9 fusion.5
  40.3 3.0 collective-permute-start.11
  45.1 2.0 bitcast_dynamic-update-slice_fusion.3
  47.3 3.2 collective-permute-start.5
  50.5 1.9 collective-permute-start.6
  52.4 2.7 collective-permute-start.7
  56.7 2.4 collective-permute-done.6
  59.2 5.6 %collective-permute-done.7 = bf16[256,4,128]{2,0,1:T(8,128)(2,1)S(1)} collective-permute-done((bf16[256,4,128]{2,0,1:T(8,128)(2,1)S(1)}, bf16[256,4,128]{2,0,1:T(8,128)(2,1)S(1)}, u32[]{:S(2)}, u32[]{:S(2)}) %collective-permute-start.7) | collective-permute-done | bytes 262176 | tf_op jit(solution)/shard_map/ppermute | solution.py:14
  64.8 3.2 collective-permute-done.8
  69.8 5.4 %fusion.22 = f32[256,4096]{1,0:T(8,128)} fusion(bf16[512,4096]{1,0:T(8,128)(2,1)} %param.21, bf16[32,8,4,128]{3,2,1,0:T(4,128)(2,1)S(1)} %bitcast.136), kind=kOutput, calls=%fused_computation.45 | convolution fusion | flops 1073741824 | bytes 8650752 | tf_op jit(solution)/shard_map/dot_general | solution.py:137
  75.2 52.2 %reduce-scatter.2.cloned.1.call-done = f32[64,4096]{1,0:T(8,128)} async-done(((f32[256,4096]{1,0:T(8,128)}), f32[64,4096]{1,0:T(8,128)}) %reduce-scatter.2.cloned.1.call-update) | async-done | bytes 1048592 | tf_op jit(solution)/shard_map/reduce_scatter | solution.py:136
  130.3 1.7 collective-permute-start.12
  132.0 14.9 %collective-permute-done.12 = bf16[64,4096]{1,0:T(8,128)(2,1)S(1)} collective-permute-done((bf16[64,4096]{1,0:T(8,128)(2,1)S(1)}, bf16[64,4096]{1,0:T(8,128)(2,1)S(1)}, u32[]{:S(2)}, u32[]{:S(2)}) %collective-permute-start.12) | collective-permute-done | bytes 524320 | tf_op jit(solution)/shard_map/ppermute | solution.py:154
  146.9 4.7 %collective-permute-start.16 = (bf16[64,4096]{1,0:T(8,128)(2,1)S(1)}, bf16[64,4096]{1,0:T(8,128)(2,1)S(1)}, u32[]{:S(2)}, u32[]{:S(2)}) collective-permute-start(bf16[64,4096]{1,0:T(8,128)(2,1)S(1)} %multiply_convert_fusion), channel_id=1, source_target_pairs={{0,28},{4,0},{8,4},{12,8},{16,12},{20,16},{24,20},{28,24},{1,29},{... | collective-permute-start | bytes 1572872 | tf_op jit(solution)/shard_map/ppermute | solution.py:156
  151.6 17.1 %collective-permute-done.13 = bf16[64,4096]{1,0:T(8,128)(2,1)S(1)} collective-permute-done((bf16[64,4096]{1,0:T(8,128)(2,1)S(1)}, bf16[64,4096]{1,0:T(8,128)(2,1)S(1)}, u32[]{:S(2)}, u32[]{:S(2)}) %collective-permute-start.13) | collective-permute-done | bytes 524320 | tf_op jit(solution)/shard_map/ppermute | solution.py:154
  168.7 2.5 collective-permute-start.14
  171.2 12.3 %collective-permute-start.17 = (bf16[64,4096]{1,0:T(8,128)(2,1)S(1)}, bf16[64,4096]{1,0:T(8,128)(2,1)S(1)}, u32[]{:S(2)}, u32[]{:S(2)}) collective-permute-start(bf16[64,4096]{1,0:T(8,128)(2,1)S(1)} %collective-permute-done.16), channel_id=1, source_target_pairs={{0,28},{4,0},{8,4},{12,8},{16,12},{20,16},{24,20},{28,24},{1,29},{... | collective-permute-start | bytes 1572872 | tf_op jit(solution)/shard_map/ppermute | solution.py:156
  183.6 8.7 %collective-permute-done.14 = bf16[64,4096]{1,0:T(8,128)(2,1)S(1)} collective-permute-done((bf16[64,4096]{1,0:T(8,128)(2,1)S(1)}, bf16[64,4096]{1,0:T(8,128)(2,1)S(1)}, u32[]{:S(2)}, u32[]{:S(2)}) %collective-permute-start.14) | collective-permute-done | bytes 524320 | tf_op jit(solution)/shard_map/ppermute | solution.py:154
  192.2 2.5 collective-permute-start.15
  196.9 16.6 %all-reduce = s32[512]{0:T(512)S(1)} all-reduce(s32[512]{0:T(512)S(1)} %dynamic-update-slice), channel_id=1, replica_groups=mesh['req'=8,'mp'=4] {'req'}, use_global_device_ids=true, to_apply=%add | all-reduce | flops 512 | bytes 4096
  215.5 10.1 %collective-permute-done.18 = bf16[64,4096]{1,0:T(8,128)(2,1)S(1)} collective-permute-done((bf16[64,4096]{1,0:T(8,128)(2,1)S(1)}, bf16[64,4096]{1,0:T(8,128)(2,1)S(1)}, u32[]{:S(2)}, u32[]{:S(2)}) %collective-permute-start.18) | collective-permute-done | bytes 524320 | tf_op jit(solution)/shard_map/ppermute | solution.py:156
  227.0 23.7 %fusion.38 = (f32[512]{0:T(512)S(1)}, f32[512,4000]{0,1:T(8,128)}) fusion(bf16[4096,4000]{0,1:T(8,128)(2,1)} %param.23, bf16[1024,4096]{1,0:T(8,128)(2,1)S(1)} %constant_dynamic-update-slice_fusion.10, s32[]{:T(128)S(6)} %select_n.205), kind=kOutput, calls=%fused_computation.121 | convolution fusion | flops 16779264000 | bytes 45156356 | tf_op jit(solution)/shard_map/dot_general | solution.py:160
  250.8 4.8 %multiply_reduce_fusion = (f32[512]{0:T(512)S(1)}, f32[512]{0:T(512)S(1)}, f32[512]{0:T(512)S(1)}) fusion(f32[512,4000]{0,1:T(8,128)} %get-tuple-element.271, f32[512]{0:T(512)S(1)} %get-tuple-element.270, s32[512]{0:T(512)S(1)} %broadcast_subtract_fusion), kind=kLoop, calls=%fused_computation.13 | loop fusion | flops 14334464 | bytes 8202240 | tf_op jit(solution)/shard_map/reduce_sum | solution.py:164
  255.7 30.4 %all_gather.19 = f32[8,8,64]{2,1,0:T(8,128)S(1)} all-gather(f32[1,8,64]{2,1,0:T(8,128)S(1)} %all_gather_reshape.15), channel_id=1, replica_groups=mesh['req'=8,'mp'=4] {'req'}, dimensions={0}, use_global_device_ids=true | all-gather | bytes 18432 | tf_op jit(solution)/shard_map/all_gather | solution.py:18
  286.2 30.4 %all_gather.17 = f32[8,8,64]{2,1,0:T(8,128)S(1)} all-gather(f32[1,8,64]{2,1,0:T(8,128)S(1)} %all_gather_reshape.14), channel_id=1, replica_groups=mesh['req'=8,'mp'=4] {'req'}, dimensions={0}, use_global_device_ids=true | all-gather | bytes 18432 | tf_op jit(solution)/shard_map/all_gather | solution.py:18
  316.6 30.4 %all_gather.16 = f32[8,8,64]{2,1,0:T(8,128)S(1)} all-gather(f32[1,8,64]{2,1,0:T(8,128)S(1)} %all_gather_reshape.13), channel_id=1, replica_groups=mesh['req'=8,'mp'=4] {'req'}, dimensions={0}, use_global_device_ids=true | all-gather | bytes 18432 | tf_op jit(solution)/shard_map/all_gather | solution.py:18
  347.1 30.4 %all_gather.15 = f32[8,8,64]{2,1,0:T(8,128)S(1)} all-gather(f32[1,8,64]{2,1,0:T(8,128)S(1)} %all_gather_reshape.12), channel_id=1, replica_groups=mesh['req'=8,'mp'=4] {'req'}, dimensions={0}, use_global_device_ids=true | all-gather | bytes 18432 | tf_op jit(solution)/shard_map/all_gather | solution.py:18
  (120 shorter events, 21.9 us)
Async XLA Ops:
  7.2 8.6 %copy-start = (bf16[2048,2,128]{2,1,0:T(2,128)(2,1)S(1)}, bf16[2048,2,128]{2,1,0:T(2,128)(2,1)}, u32[]{:S(2)}) copy-start(bf16[2048,2,128]{2,1,0:T(2,128)(2,1)} %param.19) | copy-start | bytes 3145732
  7.2 28.5 %copy-start.3 = (bf16[256,512]{1,0:T(8,128)(2,1)S(1)}, bf16[256,512]{1,0:T(8,128)(2,1)}, u32[]{:S(2)}) copy-start(bf16[256,512]{1,0:T(8,128)(2,1)} %param.16) | copy-start | bytes 786436
  7.2 120.2 %reduce-scatter.2.cloned.1.call-start = ((), (), s32[]{:S(2)}) async-start(), calls=%async_computation.1 | async-start | bytes 5242880 | tf_op jit(solution)/shard_map/reduce_scatter | solution.py:136
  7.2 28.4 %collective-permute-start = (bf16[256,512]{1,0:T(8,128)(2,1)}, bf16[256,512]{1,0:T(8,128)(2,1)S(1)}, u32[]{:S(2)}, u32[]{:S(2)}) collective-permute-start(bf16[256,512]{1,0:T(8,128)(2,1)} %param.16), channel_id=1, source_target_pairs={{20,0},{24,4},{28,8},{0,12},{4,16},{8,20},{12,24},{16,28},{21,1},{... | collective-permute-start | bytes 786440 | tf_op jit(solution)/shard_map/ppermute | solution.py:14
  11.2 24.4 %collective-permute-start.1 = (bf16[256,512]{1,0:T(8,128)(2,1)}, bf16[256,512]{1,0:T(8,128)(2,1)S(1)}, u32[]{:S(2)}, u32[]{:S(2)}) collective-permute-start(bf16[256,512]{1,0:T(8,128)(2,1)} %param.16), channel_id=1, source_target_pairs={{24,0},{28,4},{0,8},{4,12},{8,16},{12,20},{16,24},{20,28},{25,1},{... | collective-permute-start | bytes 786440 | tf_op jit(solution)/shard_map/ppermute | solution.py:14
  12.8 22.8 %collective-permute-start.2 = (bf16[256,512]{1,0:T(8,128)(2,1)}, bf16[256,512]{1,0:T(8,128)(2,1)S(1)}, u32[]{:S(2)}, u32[]{:S(2)}) collective-permute-start(bf16[256,512]{1,0:T(8,128)(2,1)} %param.16), channel_id=1, source_target_pairs={{28,0},{0,4},{4,8},{8,12},{12,16},{16,20},{20,24},{24,28},{29,1},{... | collective-permute-start | bytes 786440 | tf_op jit(solution)/shard_map/ppermute | solution.py:14
  39.1 16.0 %collective-permute-start.9 = (f32[256,4]{0,1:T(4,128)S(1)}, f32[256,4]{0,1:T(4,128)S(1)}, u32[]{:S(2)}, u32[]{:S(2)}) collective-permute-start(f32[256,4]{0,1:T(4,128)S(1)} %get-tuple-element.260), channel_id=1, source_target_pairs={{4,0},{8,4},{12,8},{16,12},{20,16},{24,20},{28,24},{0,28},{5,1},{9... | collective-permute-start | bytes 12296 | tf_op jit(solution)/shard_map/ppermute | solution.py:14
  39.2 16.9 %collective-permute-start.10 = (f32[256,4]{0,1:T(4,128)S(1)}, f32[256,4]{0,1:T(4,128)S(1)}, u32[]{:S(2)}, u32[]{:S(2)}) collective-permute-start(f32[256,4]{0,1:T(4,128)S(1)} %get-tuple-element.259), channel_id=1, source_target_pairs={{8,0},{12,4},{16,8},{20,12},{24,16},{28,20},{0,24},{4,28},{9,1},{1... | collective-permute-start | bytes 12296 | tf_op jit(solution)/shard_map/ppermute | solution.py:14
  40.3 15.8 %collective-permute-start.11 = (f32[256,4]{0,1:T(4,128)S(1)}, f32[256,4]{0,1:T(4,128)S(1)}, u32[]{:S(2)}, u32[]{:S(2)}) collective-permute-start(f32[256,4]{0,1:T(4,128)S(1)} %get-tuple-element.258), channel_id=1, source_target_pairs={{12,0},{16,4},{20,8},{24,12},{28,16},{0,20},{4,24},{8,28},{13,1},{... | collective-permute-start | bytes 12296 | tf_op jit(solution)/shard_map/ppermute | solution.py:14
  43.3 4.0 %collective-permute-start.3 = (f32[256,4]{0,1:T(4,128)S(1)}, f32[256,4]{0,1:T(4,128)S(1)}, u32[]{:S(2)}, u32[]{:S(2)}) collective-permute-start(f32[256,4]{0,1:T(4,128)S(1)} %get-tuple-element.263), channel_id=1, source_target_pairs={{4,0},{8,4},{12,8},{16,12},{20,16},{24,20},{28,24},{0,28},{5,1},{9... | collective-permute-start | bytes 12296 | tf_op jit(solution)/shard_map/ppermute | solution.py:14
  44.8 5.7 %collective-permute-start.4 = (f32[256,4]{0,1:T(4,128)S(1)}, f32[256,4]{0,1:T(4,128)S(1)}, u32[]{:S(2)}, u32[]{:S(2)}) collective-permute-start(f32[256,4]{0,1:T(4,128)S(1)} %get-tuple-element.262), channel_id=1, source_target_pairs={{8,0},{12,4},{16,8},{20,12},{24,16},{28,20},{0,24},{4,28},{9,1},{1... | collective-permute-start | bytes 12296 | tf_op jit(solution)/shard_map/ppermute | solution.py:14
  47.3 5.1 %collective-permute-start.5 = (f32[256,4]{0,1:T(4,128)S(1)}, f32[256,4]{0,1:T(4,128)S(1)}, u32[]{:S(2)}, u32[]{:S(2)}) collective-permute-start(f32[256,4]{0,1:T(4,128)S(1)} %get-tuple-element.261), channel_id=1, source_target_pairs={{12,0},{16,4},{20,8},{24,12},{28,16},{0,20},{4,24},{8,28},{13,1},{... | collective-permute-start | bytes 12296 | tf_op jit(solution)/shard_map/ppermute | solution.py:14
  50.5 8.7 %collective-permute-start.6 = (bf16[256,4,128]{2,0,1:T(8,128)(2,1)S(1)}, bf16[256,4,128]{2,0,1:T(8,128)(2,1)S(1)}, u32[]{:S(2)}, u32[]{:S(2)}) collective-permute-start(bf16[256,4,128]{2,0,1:T(8,128)(2,1)S(1)} %get-tuple-element.255), channel_id=1, source_target_pairs={{4,0},{8,4},{12,8},{16,12},{20,16},{24,20},{28,24},{0,28},{5,1},{9... | collective-permute-start | bytes 786440 | tf_op jit(solution)/shard_map/ppermute | solution.py:14
  52.4 12.4 %collective-permute-start.7 = (bf16[256,4,128]{2,0,1:T(8,128)(2,1)S(1)}, bf16[256,4,128]{2,0,1:T(8,128)(2,1)S(1)}, u32[]{:S(2)}, u32[]{:S(2)}) collective-permute-start(bf16[256,4,128]{2,0,1:T(8,128)(2,1)S(1)} %get-tuple-element.254), channel_id=1, source_target_pairs={{8,0},{12,4},{16,8},{20,12},{24,16},{28,20},{0,24},{4,28},{9,1},{1... | collective-permute-start | bytes 786440 | tf_op jit(solution)/shard_map/ppermute | solution.py:14
  55.1 12.9 %collective-permute-start.8 = (bf16[256,4,128]{2,0,1:T(8,128)(2,1)S(1)}, bf16[256,4,128]{2,0,1:T(8,128)(2,1)S(1)}, u32[]{:S(2)}, u32[]{:S(2)}) collective-permute-start(bf16[256,4,128]{2,0,1:T(8,128)(2,1)S(1)} %get-tuple-element.253), channel_id=1, source_target_pairs={{12,0},{16,4},{20,8},{24,12},{28,16},{0,20},{4,24},{8,28},{13,1},{... | collective-permute-start | bytes 786440 | tf_op jit(solution)/shard_map/ppermute | solution.py:14
  69.4 58.0 %copy-start.2 = (bf16[64,4096]{1,0:T(8,128)(2,1)S(1)}, bf16[64,4096]{1,0:T(8,128)(2,1)}, u32[]{:S(2)}) copy-start(bf16[64,4096]{1,0:T(8,128)(2,1)} %param.15) | copy-start | bytes 1572868
  69.8 59.1 %copy-start.4 = (f32[4096]{0:T(1024)S(1)}, f32[4096]{0:T(1024)}, u32[]{:S(2)}) copy-start(f32[4096]{0:T(1024)} %param.22) | copy-start | bytes 49156
  69.8 125.6 %copy-start.6 = (u32[32]{0:T(128)S(1)}, u32[32]{0:T(128)}, u32[]{:S(2)}) copy-start(u32[32]{0:T(128)} %constant.144) | copy-start | bytes 388
  69.8 126.8 %copy-start.5 = (s32[64]{0:T(128)S(1)}, s32[64]{0:T(128)}, u32[]{:S(2)}) copy-start(s32[64]{0:T(128)} %param.24) | copy-start | bytes 772
  130.3 16.6 %collective-permute-start.12 = (bf16[64,4096]{1,0:T(8,128)(2,1)S(1)}, bf16[64,4096]{1,0:T(8,128)(2,1)S(1)}, u32[]{:S(2)}, u32[]{:S(2)}) collective-permute-start(bf16[64,4096]{1,0:T(8,128)(2,1)S(1)} %multiply_convert_fusion), channel_id=1, source_target_pairs={{0,4},{4,8},{8,12},{12,16},{16,20},{20,24},{24,28},{28,0},{1,5},{5... | collective-permute-start | bytes 1572872 | tf_op jit(solution)/shard_map/ppermute | solution.py:154
  146.9 21.8 %collective-permute-start.13 = (bf16[64,4096]{1,0:T(8,128)(2,1)S(1)}, bf16[64,4096]{1,0:T(8,128)(2,1)S(1)}, u32[]{:S(2)}, u32[]{:S(2)}) collective-permute-start(bf16[64,4096]{1,0:T(8,128)(2,1)S(1)} %collective-permute-done.12), channel_id=1, source_target_pairs={{0,4},{4,8},{8,12},{12,16},{16,20},{20,24},{24,28},{28,0},{1,5},{5... | collective-permute-start | bytes 1572872 | tf_op jit(solution)/shard_map/ppermute | solution.py:154
  146.9 24.3 %collective-permute-start.16 = (bf16[64,4096]{1,0:T(8,128)(2,1)S(1)}, bf16[64,4096]{1,0:T(8,128)(2,1)S(1)}, u32[]{:S(2)}, u32[]{:S(2)}) collective-permute-start(bf16[64,4096]{1,0:T(8,128)(2,1)S(1)} %multiply_convert_fusion), channel_id=1, source_target_pairs={{0,28},{4,0},{8,4},{12,8},{16,12},{20,16},{24,20},{28,24},{1,29},{... | collective-permute-start | bytes 1572872 | tf_op jit(solution)/shard_map/ppermute | solution.py:156
  168.7 23.5 %collective-permute-start.14 = (bf16[64,4096]{1,0:T(8,128)(2,1)S(1)}, bf16[64,4096]{1,0:T(8,128)(2,1)S(1)}, u32[]{:S(2)}, u32[]{:S(2)}) collective-permute-start(bf16[64,4096]{1,0:T(8,128)(2,1)S(1)} %collective-permute-done.13), channel_id=1, source_target_pairs={{0,4},{4,8},{8,12},{12,16},{16,20},{20,24},{24,28},{28,0},{1,5},{5... | collective-permute-start | bytes 1572872 | tf_op jit(solution)/shard_map/ppermute | solution.py:154
  171.2 42.3 %collective-permute-start.17 = (bf16[64,4096]{1,0:T(8,128)(2,1)S(1)}, bf16[64,4096]{1,0:T(8,128)(2,1)S(1)}, u32[]{:S(2)}, u32[]{:S(2)}) collective-permute-start(bf16[64,4096]{1,0:T(8,128)(2,1)S(1)} %collective-permute-done.16), channel_id=1, source_target_pairs={{0,28},{4,0},{8,4},{12,8},{16,12},{20,16},{24,20},{28,24},{1,29},{... | collective-permute-start | bytes 1572872 | tf_op jit(solution)/shard_map/ppermute | solution.py:156
  192.2 21.9 %collective-permute-start.15 = (bf16[64,4096]{1,0:T(8,128)(2,1)S(1)}, bf16[64,4096]{1,0:T(8,128)(2,1)}, u32[]{:S(2)}, u32[]{:S(2)}) collective-permute-start(bf16[64,4096]{1,0:T(8,128)(2,1)S(1)} %collective-permute-done.14), channel_id=1, source_target_pairs={{0,4},{4,8},{8,12},{12,16},{16,20},{20,24},{24,28},{28,0},{1,5},{5... | collective-permute-start | bytes 1572872 | tf_op jit(solution)/shard_map/ppermute | solution.py:154
  213.5 12.0 %collective-permute-start.18 = (bf16[64,4096]{1,0:T(8,128)(2,1)S(1)}, bf16[64,4096]{1,0:T(8,128)(2,1)S(1)}, u32[]{:S(2)}, u32[]{:S(2)}) collective-permute-start(bf16[64,4096]{1,0:T(8,128)(2,1)S(1)} %collective-permute-done.17), channel_id=1, source_target_pairs={{0,28},{4,0},{8,4},{12,8},{16,12},{20,16},{24,20},{28,24},{1,29},{... | collective-permute-start | bytes 1572872 | tf_op jit(solution)/shard_map/ppermute | solution.py:156
  227.0 151.5 %copy-start.1 = (bf16[2048,2,128]{2,1,0:T(2,128)(2,1)S(1)}, bf16[2048,2,128]{2,1,0:T(2,128)(2,1)}, u32[]{:S(2)}) copy-start(bf16[2048,2,128]{2,1,0:T(2,128)(2,1)} %param.19) | copy-start | bytes 3145732
Sparse Core Ops, SparseCore 0:
  75.4 51.9 reduce-scatter.1
